TPU v7x, 256 devices: a whole 4x4x8 slice. The times are simulated.
256 devices in a mesh: dp: 32 (over x_lo, z, core), expert: 8 (over x_hi, y).
Axes of the slice: x: 4 (x_hi: 2, x_lo: 2; x = x_hi * 2 + x_lo), y: 4, z: 8, core: 2. Of those that a mesh axis runs over, the one named last changes fastest.
Arguments:
- tokens: bfloat16 [49152, 4096], P(('dp', 'expert')), may hold values from -24 to 24
- routes: int32 [49152, 2], P(('dp', 'expert')), may hold values from 0 to 7, all different within a row; in each aligned block of 192 rows (0 to 191, 192 to 383, ...) at most 64 rows name the same one
- positives: int32 [512], P(('dp', 'expert')), may hold values from 0 to 511, each once
- expert_out: bfloat16 [32, 8, 8, 64, 4096], P('dp', 'expert'), may hold values from -6 to 6
- router: bfloat16 [4096, 8], replicated, may hold values from -0.09375 to 0.09375
- norm_gain: float32 [4096], replicated, may hold values from 0.25 to 1.75
- loss_scale: float32 [], replicated, may hold values from 8192 to 65536
Outputs:
- token_grad: bfloat16 [49152, 4096], P(('dp', 'expert'))
- expert_grad: bfloat16 [32, 8, 8, 64, 4096], P('dp', 'expert')
- router_grad: float32 [4096, 8], replicated
- loss: float32 [], replicated
Inputs may be any that keep to these rules, and one draw needn't show every extreme that they name: `routes`: each row names 2 different experts; among the rows of one device no expert is named by more than 64 rows, a bound that some block reaches. `positives`: A permutation of the records.
All inputs are finite; a program needn't handle non-finite values.
Results may differ from a plain program's by a relative error of at most 0.0061.
Values may be sent and summed in bfloat16 or wider, within the bound.
No kernel may reach another device: no remote copies, remote signals or barrier semaphores. Data moves between devices by JAX's collectives and lax.ppermute only.
A program may use at most 128 MiB of HBM per device.

v0:
```python
import math
import jax
import jax.numpy as jnp
from jax import lax
from jax.sharding import PartitionSpec as P

PAIR_DEV = 2
SEQ = 48
norm_eps = 1e-05


def slot_where(routes, experts, capacity):
    hit_table = (routes[:, :, None] == jnp.arange(experts, dtype=jnp.int32)[None, None, :]).astype(
        jnp.int32
    )
    flat_hits = hit_table.reshape(-1, experts)
    before = jnp.cumsum(flat_hits, axis=0) - flat_hits
    slot_rank = jnp.sum(before * flat_hits, axis=1).reshape(routes.shape)
    return routes * capacity + slot_rank


def forward_rows(tokens, routes, received, router, norm_gain):
    experts = received.shape[0]
    capacity = received.shape[1]
    hidden_width = received.shape[2]
    logits = jnp.dot(tokens, router, preferred_element_type=jnp.float32)
    one_hot = (routes[:, :, None] == jnp.arange(experts, dtype=jnp.int32)[None, None, :]).astype(
        jnp.float32
    )
    chosen = jnp.sum(one_hot * logits[:, None, :], axis=2)
    gate_mix = jax.nn.softmax(chosen, axis=1)
    slot_rows = slot_where(routes, experts, capacity)
    fetched = received.reshape(experts * capacity, hidden_width)[slot_rows]
    summed_rows = (
        tokens.astype(jnp.float32)
        + gate_mix[:, 0:1] * fetched[:, 0].astype(jnp.float32)
        + gate_mix[:, 1:2] * fetched[:, 1].astype(jnp.float32)
    )
    inverse = lax.rsqrt(jnp.mean(summed_rows * summed_rows, axis=1, keepdims=True) + norm_eps)
    normed = summed_rows * inverse * norm_gain
    pooled = jnp.mean(normed.reshape(-1, SEQ, hidden_width), axis=1).astype(jnp.bfloat16)
    return (pooled, (gate_mix, one_hot, slot_rows, fetched, summed_rows, inverse))


def backward_rows(tokens, router, norm_gain, saved, grad_pool, experts, capacity):
    gate_mix, one_hot, slot_rows, fetched, summed_rows, inverse = saved
    hidden_width = tokens.shape[1]
    grad_rows = jnp.broadcast_to(
        grad_pool[:, None, :] / SEQ, (grad_pool.shape[0], SEQ, hidden_width)
    ).reshape(-1, hidden_width)
    weighted = grad_rows * norm_gain
    grad_summed = inverse * weighted - summed_rows * inverse**3 * jnp.mean(
        weighted * summed_rows, axis=1, keepdims=True
    )
    grad_gate = jnp.sum(grad_summed[:, None, :] * fetched.astype(jnp.float32), axis=2)
    grad_chosen = gate_mix * (grad_gate - jnp.sum(gate_mix * grad_gate, axis=1, keepdims=True))
    grad_logits = jnp.sum(one_hot * grad_chosen[:, :, None], axis=1).astype(jnp.bfloat16)
    router_part = lax.dot_general(
        tokens, grad_logits, (((0,), (0,)), ((), ())), preferred_element_type=jnp.float32
    )
    through_router = lax.dot_general(
        grad_logits, router, (((1,), (1,)), ((), ())), preferred_element_type=jnp.float32
    )
    token_grad = (grad_summed + through_router).astype(jnp.bfloat16)
    outgoing = (
        (gate_mix[:, :, None] * grad_summed[:, None, :])
        .astype(jnp.bfloat16)
        .reshape(-1, hidden_width)
    )
    sendback = (
        jnp.zeros((experts * capacity, hidden_width), jnp.bfloat16)
        .at[slot_rows.reshape(-1)]
        .set(outgoing)
    )
    return (token_grad, sendback.reshape(experts, capacity, hidden_width), router_part)


def score_rows(queries, records_all, positives, loss_scale, pair_total, score_scale):
    scores = (
        lax.dot_general(
            queries, records_all, (((1,), (1,)), ((), ())), preferred_element_type=jnp.float32
        )
        * score_scale
    )
    highest = jnp.max(scores, axis=1, keepdims=True)
    log_total = highest[:, 0] + jnp.log(jnp.sum(jnp.exp(scores - highest), axis=1))
    is_positive = jnp.arange(pair_total, dtype=jnp.int32)[None, :] == positives[:, None]
    positive_score = jnp.sum(jnp.where(is_positive, scores, jnp.zeros_like(scores)), axis=1)
    row_loss = log_total - positive_score
    softmax_rows = jnp.exp(scores - log_total[:, None])
    score_grad = (
        (softmax_rows - is_positive.astype(jnp.float32)) * (loss_scale / pair_total)
    ).astype(jnp.bfloat16)
    return (row_loss, score_grad)


def shards(tokens, routes, positives, expert_out, router, norm_gain, loss_scale):
    experts = expert_out.shape[2]
    capacity = expert_out.shape[3]
    hidden_width = expert_out.shape[4]
    received = lax.all_to_all(
        expert_out.reshape(experts, capacity, hidden_width),
        "expert",
        split_axis=0,
        concat_axis=0,
        tiled=True,
    )
    pooled, saved = forward_rows(tokens, routes, received, router, norm_gain)
    queries = pooled[:PAIR_DEV]
    records = pooled[PAIR_DEV:]
    loop_size = lax.axis_size("dp")
    column_size = lax.axis_size("expert")
    device_count = loop_size * column_size
    pair_total = PAIR_DEV * device_count
    score_scale = 4.0 / math.sqrt(hidden_width)
    records_all = lax.all_gather(records, ("dp", "expert"), axis=0, tiled=True)
    row_loss, score_grad = score_rows(
        queries, records_all, positives, loss_scale, pair_total, score_scale
    )
    loss_local = jnp.sum(row_loss)
    grad_queries = (
        jnp.dot(score_grad, records_all, preferred_element_type=jnp.float32) * score_scale
    )
    grad_records = lax.psum_scatter(
        lax.dot_general(
            score_grad, queries, (((0,), (0,)), ((), ())), preferred_element_type=jnp.float32
        )
        * score_scale,
        ("dp", "expert"),
        scatter_dimension=0,
        tiled=True,
    )
    grad_pool = jnp.concatenate([grad_queries, grad_records], axis=0)
    token_grad, sendback, router_part = backward_rows(
        tokens, router, norm_gain, saved, grad_pool, experts, capacity
    )
    returned = lax.all_to_all(sendback, "expert", split_axis=0, concat_axis=0, tiled=True)
    router_grad, loss_total = lax.psum((router_part, loss_local), ("dp", "expert"))
    expert_grad = returned.reshape(1, 1, experts, capacity, hidden_width)
    return (token_grad, expert_grad, router_grad, loss_total / pair_total)


def solution(mesh):
    placed = (
        P(("dp", "expert"), None),
        P(("dp", "expert"), None),
        P(("dp", "expert")),
        P("dp", "expert", None, None, None),
        P(),
        P(),
        P(),
    )
    return jax.shard_map(
        shards,
        mesh=mesh,
        in_specs=placed,
        out_specs=(P(("dp", "expert"), None), P("dp", "expert", None, None, None), P(), P()),
        check_vma=False,
    )
```

profile of v0, /device:TPU:8, one launch (start us, length us, event | category | flops | bytes accessed | tf_op | source)
XLA Modules:
  0.0 1506.5 jit_solution(1943185011051784695)
XLA Ops:
  7.2 0.0 copy-start
  7.2 0.0 copy-start.8
  7.2 0.0 copy-start.4
  7.2 7.5 all-to-all-start
  14.7 0.0 all-gather.3.cloned.1.call-start
  14.7 0.1 copy.45
  14.9 0.1 eq.59
  15.0 0.1 eq.55
  15.2 0.9 reduce-window.6
  16.0 0.2 slice_reduce_fusion
  16.3 0.1 fusion.7
  16.4 0.1 reshape.211
  16.5 0.1 copy.47
  16.6 0.1 copy.48
  16.8 0.1 reshape.221
  16.9 0.0 copy-done
  16.9 0.0 copy-done.4
  16.9 0.5 fusion.20
  17.5 45.7 %all-to-all-done = bf16[8,64,4096]{2,1,0:T(8,128)(2,1)} async-done(((bf16[8,64,4096]{2,1,0:T(8,128)(2,1)}), bf16[8,64,4096]{2,1,0:T(8,128)(2,1)}, u32[]{:S(2)}, u32[]{:S(2)}) %all-to-all-start) | async-done | bytes 4194336 | tf_op jit(solution)/shard_map/all_to_all | solution.py:101
  63.2 11.0 gather_fusion
  74.2 4.6 reshape.220
  78.8 0.0 copy-start.5
  78.8 7.0 fusion.17
  85.8 0.0 copy-start.6
  85.8 4.0 multiply_reduce_fusion.2
  89.9 2.4 multiply_multiply_fusion
  92.3 0.2 copy-done.2
  92.5 2.2 reduce_sum.112
  94.7 0.6 slice_bitcast_fusion
  95.3 0.0 all-gather.3.cloned.1.call-update
  95.3 0.2 all-reduce.6.cloned.1.call-start
  96.2 680.8 %all-gather.3.cloned.1.call-done = bf16[256,2,4096]{2,1,0:T(2,128)(2,1)} async-done(((bf16[1,2,4096]{2,1,0:T(2,128)(2,1)}), bf16[256,2,4096]{2,1,0:T(2,128)(2,1)}) %all-gather.3.cloned.1.call-update) | async-done | bytes 4194320 | tf_op jit(solution)/shard_map/all_gather | solution.py:116
  777.0 7.2 reshape.238
  784.2 3.5 fusion.19
  787.7 0.2 select_reduce_fusion.2
  787.9 0.6 subtract_reduce_fusion
  788.5 4.6 convolution_multiply_fusion
  793.1 0.0 all-reduce.6.cloned.1.call-update
  793.1 0.1 copy.54
  793.3 0.1 div.48
  793.4 0.1 copy.53
  793.5 0.1 reshape.214
  793.7 2.9 convolution_multiply_fusion.1
  796.6 301.1 %all-reduce.6.cloned.1.call-done = f32[512,4096]{1,0:T(8,128)} async-done(((f32[512,4096]{1,0:T(8,128)}), f32[512,4096]{1,0:T(8,128)}) %all-reduce.6.cloned.1.call-update) | async-done | bytes 8388624
  1097.7 1.1 constant_dynamic-slice_fusion
  1098.8 0.3 bitcast_multiply_fusion
  1099.2 0.5 copy-done.3
  1099.7 0.4 multiply_reduce_fusion.1
  1100.1 0.7 multiply_subtract_fusion
  1100.8 1.7 copy-done.1
  1102.5 5.3 mul.182
  1107.8 8.4 mul.189
  1116.2 9.7 scatter_custom_fusion
  1125.9 6.8 all-to-all-start.1
  1132.6 112.4 %psum.15 = f32[]{:T(128)} all-reduce(f32[]{:T(128)} %get-tuple-element.6), channel_id=1, replica_groups=mesh['dp'=32,'expert'=8] {'dp','expert'}, use_global_device_ids=true, to_apply=%region_19.20 | all-reduce | flops 1 | bytes 8 | tf_op jit(solution)/shard_map/psum | solution.py:138
  1245.7 5.7 multiply_reduce_fusion
  1251.4 0.1 copy.52
  1251.5 2.4 convolution_bitcast_fusion
  1253.9 0.0 all-reduce.4.cloned.1.call-update
  1254.0 3.6 fusion
  1257.6 0.0 all-to-all-done.1
  1257.6 235.8 %all-reduce.4.cloned.1.call-done = f32[4096,8]{0,1:T(8,128)} async-done(((f32[4096,8]{0,1:T(8,128)}), f32[4096,8]{0,1:T(8,128)}) %all-reduce.4.cloned.1.call-update) | async-done | bytes 131088 | tf_op jit(solution)/shard_map/psum | solution.py:138
  1493.4 4.7 copy.69
  1498.2 0.7 copy.70
  (28 shorter events, 0.3 us)
Async XLA Ops:
  7.2 9.7 copy-start
  7.2 7.5 copy-start.8
  7.2 9.7 copy-start.4
  7.2 56.0 %all-to-all-start = ((bf16[8,64,4096]{2,1,0:T(8,128)(2,1)}), bf16[8,64,4096]{2,1,0:T(8,128)(2,1)}, u32[]{:S(2)}, u32[]{:S(2)}) async-start(bf16[8,64,4096]{2,1,0:T(8,128)(2,1)} %bitcast.46), calls=%async_computation | async-start | bytes 8388608 | tf_op jit(solution)/shard_map/all_to_all | solution.py:101
  14.7 762.3 %all-gather.3.cloned.1.call-start = ((), (), s32[]{:S(2)}) async-start(), calls=%async_computation.3 | async-start | bytes 4210688 | tf_op jit(solution)/shard_map/all_gather | solution.py:116
  78.8 7.0 copy-start.5
  85.8 4.1 copy-start.6
  89.8 2.6 copy-start.2
  95.3 1002.4 %all-reduce.6.cloned.1.call-start = ((), (), s32[]{:S(2)}) async-start(), calls=%async_computation.4 | async-start | bytes 16777216
  784.2 3.5 copy-start.9
  1097.7 2.0 copy-start.3
  1100.8 1.7 copy-start.1
  1125.9 131.7 %all-to-all-start.1 = ((bf16[8,64,4096]{2,1,0:T(8,128)(2,1)}), bf16[8,64,4096]{2,1,0:T(8,128)(2,1)}, u32[]{:S(2)}, u32[]{:S(2)}) async-start(bf16[8,64,4096]{2,1,0:T(8,128)(2,1)} %bitcast.44), calls=%async_computation.1 | async-start | bytes 8388608 | tf_op jit(solution)/shard_map/all_to_all | solution.py:137
  1132.6 360.8 %all-reduce.4.cloned.1.call-start = ((), (), s32[]{:S(2)}) async-start(), calls=%async_computation.2 | async-start | bytes 262144 | tf_op jit(solution)/shard_map/psum | solution.py:138
  1493.4 4.7 copy-start.7
Sparse Core Ops, SparseCore 0:
  95.4 681.5 all-gather.2
  793.3 304.4 all-reduce.5
  1254.1 239.3 all-reduce.3
where the time goes:
time: 1510 us
  waiting for transfers between devices  1260 us (83%)
  blocking collectives  112 us (7%)
  local copies, waits for them, and re-layouts  54.7 us (4%)
  other arithmetic  27.5 us (2%)
  matrix products  17.5 us (1%)
  between operations  16.5 us (1%)
    all_gather x1, waiting for transfers between devices, shards(): records_all = lax.all_gather(records, ('dp', 'expert'), axis=0, tiled=True)  681 us
    unnamed x4, waiting for transfers between devices  301 us
    psum x1, waiting for transfers between devices, shards(): lax.psum((router_part, loss_local), ('dp', 'expert'))  236 us
    psum x1, blocking collectives, shards(): lax.psum((router_part, loss_local), ('dp', 'expert'))  112 us
    all_to_all x1, waiting for transfers between devices, shards(): lax.all_to_all(expert_out.reshape(experts, capacity, hidden_width), 'expe...  45.7 us
  transfers between devices with their start and end apart: 5, of which 4 were waited for; matrix products, arithmetic and copies ran while one was open for 1% of the time, Pallas kernels for 0%

commit v1 on v0

--- a/solution.py
+++ b/solution.py
@@ -135,7 +135,7 @@
         tokens, router, norm_gain, saved, grad_pool, experts, capacity
     )
     returned = lax.all_to_all(sendback, "expert", split_axis=0, concat_axis=0, tiled=True)
-    router_grad, loss_total = lax.psum((router_part, loss_local), ("dp", "expert"))
+    router_grad, loss_total = jax.lax.psum(jax.lax.psum((router_part, loss_local), "expert"), "dp")
     expert_grad = returned.reshape(1, 1, experts, capacity, hidden_width)
     return (token_grad, expert_grad, router_grad, loss_total / pair_total)
 

time: 1510 us -> 1460 us (0.967)
  waiting for transfers between devices: 1260 us -> 1220 us
    psum x1 -> x2, waiting for transfers between devices: 236 us -> 191 us  [the longest x1 191 us: shards(): jax.lax.psum(jax.lax.psum((router_part, loss_local), 'expert'), 'dp')]
    psum x1 -> x2, blocking collectives: 112 us -> 107 us  [the longest x1 53.9 us: shards(): jax.lax.psum(jax.lax.psum((router_part, loss_local), 'expert'), 'dp')]
    unnamed x4 -> x5, waiting for transfers between devices: 301 us -> 301 us
  transfers between devices with their start and end apart: 5 -> 6, of which waited for: 4 -> 4; matrix products, arithmetic and copies ran while one was open for 1% -> 1% of each run, Pallas kernels for 0% -> 0%
where the time goes in v1:
time: 1460 us
  waiting for transfers between devices  1220 us (84%)
  blocking collectives  107 us (7%)
  local copies, waits for them, and re-layouts  54.7 us (4%)
  other arithmetic  27.5 us (2%)
  matrix products  17.5 us (1%)
  between operations  16.5 us (1%)
  starting transfers between devices  14.6 us (1%)
    all_gather x1, waiting for transfers between devices, shards(): records_all = lax.all_gather(records, ('dp', 'expert'), axis=0, tiled=True)  681 us
    unnamed x5, waiting for transfers between devices  301 us
    psum x1, waiting for transfers between devices, shards(): jax.lax.psum(jax.lax.psum((router_part, loss_local), 'expert'), 'dp')  191 us
    psum x1, blocking collectives, shards(): jax.lax.psum(jax.lax.psum((router_part, loss_local), 'expert'), 'dp')  53.9 us
    psum x1, blocking collectives, shards(): jax.lax.psum((router_part, loss_local), 'expert')  53.6 us
    all_to_all x1, waiting for transfers between devices, shards(): lax.all_to_all(expert_out.reshape(experts, capacity, hidden_width), 'expe...  45.7 us
  transfers between devices with their start and end apart: 6, of which 4 were waited for; matrix products, arithmetic and copies ran while one was open for 1% of the time, Pallas kernels for 0%

profile of v1, /device:TPU:8, one launch (start us, length us, event | category | flops | bytes accessed | tf_op | source)
XLA Modules:
  0.0 1457.3 jit_solution(15537055974868488303)
XLA Ops:
  7.2 0.0 copy-start
  7.2 0.0 copy-start.4
  7.2 7.5 all-to-all-start
  14.7 0.1 copy.45
  14.9 0.1 eq.59
  15.0 0.1 eq.55
  15.2 0.9 reduce-window.6
  16.0 0.2 slice_reduce_fusion
  16.3 0.1 fusion.7
  16.4 0.1 reshape.211
  16.5 0.1 copy.47
  16.6 0.1 copy.48
  16.7 0.1 reshape.221
  16.9 0.5 fusion.20
  17.5 45.7 %all-to-all-done = bf16[8,64,4096]{2,1,0:T(8,128)(2,1)} async-done(((bf16[8,64,4096]{2,1,0:T(8,128)(2,1)}), bf16[8,64,4096]{2,1,0:T(8,128)(2,1)}, u32[]{:S(2)}, u32[]{:S(2)}) %all-to-all-start) | async-done | bytes 4194336 | tf_op jit(solution)/shard_map/all_to_all | solution.py:101
  63.2 11.0 gather_fusion
  74.2 4.6 reshape.220
  78.8 0.0 copy-start.5
  78.8 7.0 fusion.17
  85.8 0.0 copy-start.6
  85.8 4.0 multiply_reduce_fusion.2
  89.9 2.4 multiply_multiply_fusion
  92.3 0.2 copy-done.2
  92.5 2.2 reduce_sum.112
  94.7 0.6 slice_bitcast_fusion
  95.3 0.0 all-gather.3.cloned.1.call-update
  95.3 0.2 all-reduce.9.cloned.1.call-start
  96.2 680.8 %all-gather.3.cloned.1.call-done = bf16[256,2,4096]{2,1,0:T(2,128)(2,1)} async-done(((bf16[1,2,4096]{2,1,0:T(2,128)(2,1)}), bf16[256,2,4096]{2,1,0:T(2,128)(2,1)}) %all-gather.3.cloned.1.call-update) | async-done | bytes 4194320 | tf_op jit(solution)/shard_map/all_gather | solution.py:116
  777.0 7.2 reshape.238
  784.2 3.5 fusion.19
  787.7 0.2 select_reduce_fusion.2
  787.9 0.6 subtract_reduce_fusion
  788.5 4.6 convolution_multiply_fusion
  793.1 0.0 all-reduce.9.cloned.1.call-update
  793.1 0.1 copy.54
  793.3 0.1 div.48
  793.4 0.1 copy.53
  793.5 0.1 reshape.214
  793.7 2.9 convolution_multiply_fusion.1
  796.6 301.1 %all-reduce.9.cloned.1.call-done = f32[512,4096]{1,0:T(8,128)} async-done(((f32[512,4096]{1,0:T(8,128)}), f32[512,4096]{1,0:T(8,128)}) %all-reduce.9.cloned.1.call-update) | async-done | bytes 8388624
  1097.7 1.1 constant_dynamic-slice_fusion
  1098.8 0.3 bitcast_multiply_fusion
  1099.2 0.5 copy-done.3
  1099.7 0.4 multiply_reduce_fusion.1
  1100.1 0.7 multiply_subtract_fusion
  1100.8 1.7 copy-done.1
  1102.5 5.3 mul.182
  1107.8 8.4 mul.189
  1116.2 9.7 scatter_custom_fusion
  1125.9 6.8 all-to-all-start.1
  1132.6 5.7 multiply_reduce_fusion
  1138.4 0.1 copy.52
  1138.5 2.4 convolution_bitcast_fusion
  1140.9 0.0 all-reduce.5.cloned.1.call-update
  1140.9 0.0 all-reduce.7.cloned.1.call-start
  1141.0 53.6 %psum.30 = f32[]{:T(128)} all-reduce(f32[]{:T(128)} %get-tuple-element.6), channel_id=1, replica_groups=mesh['dp'=32,'expert'=8] {'expert'}, use_global_device_ids=true, to_apply=%region_20.21 | all-reduce | flops 1 | bytes 8 | tf_op jit(solution)/shard_map/psum | solution.py:138
  1194.5 53.9 %psum.31 = f32[]{:T(128)} all-reduce(f32[]{:T(128)} %psum.30), channel_id=1, replica_groups=mesh['dp'=32,'expert'=8] {'dp'}, use_global_device_ids=true, to_apply=%region_21.22 | all-reduce | flops 1 | bytes 8 | tf_op jit(solution)/shard_map/psum | solution.py:138
  1249.1 0.0 all-reduce.5.cloned.1.call-done
  1249.1 0.0 all-reduce.7.cloned.1.call-update
  1249.1 3.6 fusion
  1252.8 0.0 all-to-all-done.1
  1252.8 191.4 %all-reduce.7.cloned.1.call-done = f32[4096,8]{0,1:T(8,128)} async-done(((f32[4096,8]{0,1:T(8,128)}), f32[4096,8]{0,1:T(8,128)}) %all-reduce.7.cloned.1.call-update) | async-done | bytes 131088 | tf_op jit(solution)/shard_map/psum | solution.py:138
  1444.2 4.7 copy.70
  1449.0 0.7 copy.71
  (32 shorter events, 0.3 us)
Async XLA Ops:
  7.2 9.7 copy-start
  7.2 7.5 copy-start.8
  7.2 9.7 copy-start.4
  7.2 56.0 %all-to-all-start = ((bf16[8,64,4096]{2,1,0:T(8,128)(2,1)}), bf16[8,64,4096]{2,1,0:T(8,128)(2,1)}, u32[]{:S(2)}, u32[]{:S(2)}) async-start(bf16[8,64,4096]{2,1,0:T(8,128)(2,1)} %bitcast.46), calls=%async_computation | async-start | bytes 8388608 | tf_op jit(solution)/shard_map/all_to_all | solution.py:101
  14.7 762.3 %all-gather.3.cloned.1.call-start = ((), (), s32[]{:S(2)}) async-start(), calls=%async_computation.4 | async-start | bytes 4210688 | tf_op jit(solution)/shard_map/all_gather | solution.py:116
  78.8 7.0 copy-start.5
  85.8 4.1 copy-start.6
  89.8 2.6 copy-start.2
  95.3 1002.4 %all-reduce.9.cloned.1.call-start = ((), (), s32[]{:S(2)}) async-start(), calls=%async_computation.5 | async-start | bytes 16777216
  784.2 3.5 copy-start.9
  1097.7 2.0 copy-start.3
  1100.8 1.7 copy-start.1
  1125.9 126.9 %all-to-all-start.1 = ((bf16[8,64,4096]{2,1,0:T(8,128)(2,1)}), bf16[8,64,4096]{2,1,0:T(8,128)(2,1)}, u32[]{:S(2)}, u32[]{:S(2)}) async-start(bf16[8,64,4096]{2,1,0:T(8,128)(2,1)} %bitcast.44), calls=%async_computation.1 | async-start | bytes 8388608 | tf_op jit(solution)/shard_map/all_to_all | solution.py:137
  1132.6 116.4 %all-reduce.5.cloned.1.call-start = ((), (), s32[]{:S(2)}) async-start(), calls=%async_computation.2 | async-start | bytes 262144 | tf_op jit(solution)/shard_map/psum | solution.py:138
  1140.9 303.3 %all-reduce.7.cloned.1.call-start = ((), (), s32[]{:S(2)}) async-start(), calls=%async_computation.3 | async-start | bytes 262144 | tf_op jit(solution)/shard_map/psum | solution.py:138
  1444.2 4.7 copy-start.7
Sparse Core Ops, SparseCore 0:
  95.4 681.5 all-gather.2
  793.3 304.4 all-reduce.8
  1141.0 96.2 all-reduce.4
  1249.2 194.9 all-reduce.6
